TPU v7x, 32 devices: a whole 2x2x4 slice. The times are simulated.
32 devices in a mesh: seq: 16 (over z, y, core), dp: 2 (over x).
Axes of the slice: x: 2, y: 2, z: 4, core: 2. Of those that a mesh axis runs over, the one named last changes fastest.
Arguments:
- layer_input: bfloat16 [2, 2048, 4096], P('dp', 'seq'), may hold values from -0.3125 to 0.3125
- scan_input: bfloat16 [2, 2048, 2048], P('dp', 'seq'), may hold values from -6 to 6
- readout: bfloat16 [2, 2048, 64], P('dp', 'seq'), may hold values from -6 to 6
- log_decay: float32 [2, 2048, 32], P('dp', 'seq'), may hold values from -1 to 0
- output_cotangent: bfloat16 [2, 2048, 2048], P('dp', 'seq'), may hold values from -0.0078125 to 0.0078125
- write_weight: float32 [4096, 64], P('dp'), may hold values from -6 to 6
- first_moment: float32 [4096, 64], P('dp'), may hold values from -6 to 6
- second_moment: float32 [4096, 64], P('dp'), may hold values from 1 to 25
Outputs:
- decay_gradient: float32 [2, 2048, 32], P('dp', 'seq')
- new_weight: float32 [4096, 64], P('dp')
- new_first: float32 [4096, 64], P('dp')
- new_second: float32 [4096, 64], P('dp')
All inputs are finite; a program needn't handle non-finite values.
Results may differ from a plain program's by a relative error of at most 0.0039.
Values may be sent and summed in bfloat16 or wider, within the bound.
A program may use at most 64 MiB of HBM per device.

v0:
```python
import jax
import jax.numpy as jnp
from jax import lax
from jax.sharding import PartitionSpec as P

HALF_HEAD_COUNT = 32
HEAD_DIM = 64
STATE = 64
beta_one = 0.9
beta_two = 0.999
adam_count = 10.0
learn_rate = 0.01
weight_decay = 0.1
epsilon = 1e-08
highest = lax.Precision.HIGHEST


def entering(part, axis, combine, identity, reverse):
    count = lax.axis_size(axis)
    place = lax.axis_index(axis)
    ahead = count - 1 - place if reverse else place
    gathered = jax.tree.map(lambda a: lax.all_gather(a, axis), part)
    state = jax.tree.map(lambda a, e: jnp.zeros_like(a) + jnp.asarray(e, a.dtype), part, identity)

    def one(lap, state):
        source = count - 1 - lap if reverse else lap
        return combine(
            state, jax.tree.map(lambda a: lax.dynamic_index_in_dim(a, source, 0, False), gathered)
        )

    return lax.fori_loop(0, ahead, one, state)


def pair_combine(earlier_pair, later_pair):
    return (
        earlier_pair[0] * later_pair[0],
        later_pair[0][:, None, None] * earlier_pair[1] + later_pair[1],
    )


def adam_update(grad_rows, weight_rows, first_rows, second_rows):
    new_first = beta_one * first_rows + (1.0 - beta_one) * grad_rows
    new_second = beta_two * second_rows + (1.0 - beta_two) * grad_rows * grad_rows
    first_hat = new_first / (1.0 - beta_one**adam_count)
    second_hat = new_second / (1.0 - beta_two**adam_count)
    new_weight = weight_rows - learn_rate * (
        first_hat / (jnp.sqrt(second_hat) + epsilon) + weight_decay * weight_rows
    )
    return (new_weight, new_first, new_second)


def on_device(
    layer_input,
    scan_input,
    readout,
    log_decay,
    output_cotangent,
    write_weight,
    first_moment,
    second_moment,
):
    input_rows = layer_input[0]
    scan_rows = scan_input[0]
    read_rows = readout[0]
    decay_rows = log_decay[0]
    back_rows = output_cotangent[0]
    length = input_rows.shape[0]
    weight_half = write_weight.astype(jnp.bfloat16)
    write_sum = jnp.dot(
        input_rows,
        lax.all_gather(weight_half, "dp", axis=0, tiled=True),
        preferred_element_type=jnp.float32,
    )
    write_half = write_sum.astype(jnp.bfloat16)
    write_float = lax.optimization_barrier(write_half).astype(jnp.float32)
    running = jnp.cumsum(decay_rows, axis=0)
    overall = running[-1]
    to_end = jnp.exp(overall[None, :] - running)
    from_start = jnp.exp(running)
    scan_split = scan_rows.reshape(length, HALF_HEAD_COUNT, HEAD_DIM)
    back_split = back_rows.reshape(length, HALF_HEAD_COUNT, HEAD_DIM)
    scan_heads = scan_split.astype(jnp.float32)
    back_heads = back_split.astype(jnp.float32)
    read_float = read_rows.astype(jnp.float32)
    state_local = jnp.einsum(
        "shp,sn->hpn", scan_heads * to_end[:, :, None], write_float, precision=highest
    )
    reverse_local = jnp.einsum(
        "shp,sn->hpn", back_heads * from_start[:, :, None], read_float, precision=highest
    )
    decay_total = jnp.exp(overall)
    identity = (
        jnp.ones((HALF_HEAD_COUNT,), jnp.float32),
        jnp.zeros((HALF_HEAD_COUNT, HEAD_DIM, STATE), jnp.float32),
    )
    state_pair = entering((decay_total, state_local), "seq", pair_combine, identity, False)
    grad_pair = entering((decay_total, reverse_local), "seq", pair_combine, identity, True)
    state_before = state_pair[1]
    grad_after = grad_pair[1]
    term_one = decay_total * jnp.sum(grad_after * state_before, axis=(1, 2))
    grad_write = jnp.einsum("hpn,sn->shp", grad_after, write_float, precision=highest)
    second_rows = to_end * jnp.sum(scan_heads * grad_write, axis=2)
    term_two = jnp.cumsum(second_rows, axis=0) - second_rows
    state_read = jnp.einsum("hpn,sn->shp", state_before, read_float, precision=highest)
    third_rows = from_start * jnp.sum(back_heads * state_read, axis=2)
    term_three = jnp.flip(jnp.cumsum(jnp.flip(third_rows, 0), axis=0), 0)
    crossed = jnp.einsum("thp,shp->hts", scan_split, back_split, preferred_element_type=jnp.float32)
    heads_running = running.T
    spread = heads_running[:, None, :] - heads_running[:, :, None]
    row_index = lax.broadcasted_iota(jnp.int32, (length, length), 0)
    col_index = lax.broadcasted_iota(jnp.int32, (length, length), 1)
    kernel_mat = (
        jnp.where((row_index <= col_index)[None], jnp.exp(jnp.minimum(spread, 0.0)), 0.0) * crossed
    )
    write_read = jnp.dot(write_half, read_rows.T, preferred_element_type=jnp.float32)
    pairing = jnp.where((row_index < col_index)[None], kernel_mat * write_read[None], 0.0)
    balance = (jnp.sum(pairing, axis=2) - jnp.sum(pairing, axis=1)).T
    term_four = jnp.cumsum(balance, axis=0) - balance
    decay_grad = term_one[None, :] + term_two + term_three + term_four
    scaled_scan = (scan_heads * to_end[:, :, None]).reshape(length, HALF_HEAD_COUNT * HEAD_DIM)
    write_grad = jnp.dot(
        scaled_scan, grad_after.reshape(HALF_HEAD_COUNT * HEAD_DIM, STATE), precision=highest
    )
    write_grad = write_grad + jnp.dot(jnp.sum(kernel_mat, axis=0), read_float, precision=highest)
    grad_half = write_grad.astype(jnp.bfloat16)
    partial_grad = jnp.dot(input_rows.T, grad_half, preferred_element_type=jnp.float32)
    owner_grad = lax.psum_scatter(partial_grad, "dp", scatter_dimension=0, tiled=True)
    grad_rows = lax.psum(owner_grad, "seq")
    new_weight, new_first, new_second = adam_update(
        grad_rows, write_weight, first_moment, second_moment
    )
    return (decay_grad[None], new_weight, new_first, new_second)


def solution(mesh):
    in_specs = (
        P("dp", "seq", None),
        P("dp", "seq", None),
        P("dp", "seq", None),
        P("dp", "seq", None),
        P("dp", "seq", None),
        P("dp", None),
        P("dp", None),
        P("dp", None),
    )
    out_specs = (P("dp", "seq", None), P("dp", None), P("dp", None), P("dp", None))
    return jax.shard_map(
        on_device, mesh=mesh, in_specs=in_specs, out_specs=out_specs, check_vma=False
    )
```

profile of v0, /device:TPU:29, one launch (start us, length us, event | category | flops | bytes accessed | tf_op | source)
XLA Modules:
  0.0 436.1 jit_solution(12412782208266294412)
XLA Ops:
  7.2 0.9 copy.43
  8.4 1.3 copy.44
  9.8 1.6 fusion.17
  11.9 7.8 %all_gather.24 = bf16[4096,64]{0,1:T(8,128)(2,1)S(1)} all-gather(bf16[2048,64]{0,1:T(8,128)(2,1)S(1)} %convert_element_type.22), channel_id=1, replica_groups=mesh['seq'=16,'dp'=2] {'dp'}, dimensions={0}, use_global_device_ids=true | all-gather | bytes 786432 | tf_op jit(solution)/shard_map/all_gather | solution.py:71
  20.3 18.4 %all-gather.2 = f32[16,1,32]{2,1,0:T(1,128)S(1)} all-gather(f32[1,1,32]{2,1,0:T(1,128)S(1)} %get-tuple-element.175), channel_id=1, replica_groups=mesh['seq'=16,'dp'=2] {'seq'}, dimensions={0}, use_global_device_ids=true | all-gather | bytes 2176 | tf_op jit(solution)/shard_map/all_gather | solution.py:22
  38.9 1.8 fusion
  40.8 95.8 %all-gather.6.cloned.1.call-done = f32[512,64,64]{2,1,0:T(8,128)} async-done(((f32[32,64,64]{2,1,0:T(8,128)}), f32[512,64,64]{2,1,0:T(8,128)}) %all-gather.6.cloned.1.call-update) | async-done | bytes 8388624 | tf_op jit(solution)/shard_map/all_gather | solution.py:22
  137.4 1.9 fusion.7
  139.5 1.3 convolution_bitcast_fusion
  140.9 42.5 %reduce-scatter.2.cloned.1.call-done = f32[2048,64]{0,1:T(8,128)} async-done(((f32[4096,64]{0,1:T(8,128)}), f32[2048,64]{0,1:T(8,128)}) %reduce-scatter.2.cloned.1.call-update) | async-done | bytes 524304 | tf_op jit(solution)/shard_map/reduce_scatter | solution.py:127
  183.4 1.6 fusion.4
  185.8 90.6 %all-reduce.2.cloned.1.call-done = f32[2048,64]{0,1:T(8,128)} async-done(((f32[2048,64]{0,1:T(8,128)}), f32[2048,64]{0,1:T(8,128)}) %all-reduce.2.cloned.1.call-update) | async-done | bytes 524304 | tf_op jit(solution)/shard_map/psum | solution.py:128
  276.4 2.7 multiply_subtract_fusion
  279.2 125.0 %all-gather.8.cloned.1.call-done = f32[512,64,64]{2,1,0:T(8,128)} async-done(((f32[32,64,64]{2,1,0:T(8,128)}), f32[512,64,64]{2,1,0:T(8,128)}) %all-gather.8.cloned.1.call-update) | async-done | bytes 8388624 | tf_op jit(solution)/shard_map/all_gather | solution.py:22
  404.3 22.4 %while.27 = (s32[]{:T(128)}, f32[32,64,64]{2,1,0:T(8,128)S(1)}, s32[]{:T(128)}, f32[16,32]{1,0:T(8,128)S(1)}, f32[16,32,64,64]{3,2,1,0:T(8,128)}, /*index=5*/s32[]{:T(128)}, s32[]{:T(128)}, s32[]{:T(128)}) while((s32[]{:T(128)}, f32[32,64,64]{2,1,0:T(8,128)S(1)}, s32[]{:T(128)}, f32[16,32]{1,0:T(8,128)S(1)}, f32[16,32,64,64]{3,2,1,0:T(8,128)}, ...), condition=%wide.region_4.5_spmd, body=%wide.region_3.4_spmd.sunk | while | flops 262149 | bytes 1573375 | solution.py:31
  404.3 1.4 bitcast_add_fusion.5
  405.8 1.4 bitcast_add_fusion.5
  407.3 1.4 bitcast_add_fusion.5
  408.8 1.4 bitcast_add_fusion.5
  410.3 1.4 bitcast_add_fusion.5
  411.8 1.4 bitcast_add_fusion.5
  413.3 1.4 bitcast_add_fusion.5
  414.8 1.4 bitcast_add_fusion.5
  416.3 1.4 bitcast_add_fusion.5
  417.8 1.4 bitcast_add_fusion.5
  419.3 1.4 bitcast_add_fusion.5
  420.8 1.4 bitcast_add_fusion.5
  422.3 1.4 bitcast_add_fusion.5
  423.8 1.4 bitcast_add_fusion.5
  425.3 1.4 bitcast_add_fusion.5
  427.1 0.7 copy-done.2
  428.9 0.7 add_bitcast_fusion
  (68 shorter events, 5.1 us)
Async XLA Ops:
  7.2 12.6 %copy-start = (bf16[1,128,4096]{2,1,0:T(8,128)(2,1)S(1)}, bf16[1,128,4096]{2,1,0:T(8,128)(2,1)}, u32[]{:S(2)}) copy-start(bf16[1,128,4096]{2,1,0:T(8,128)(2,1)} %param.12) | copy-start | bytes 3145732
  7.2 2.6 copy-start.5
  7.2 129.4 %all-gather.6.cloned.1.call-start = ((), (), s32[]{:S(2)}) async-start(), calls=%async_computation.3 | async-start | bytes 17825792 | tf_op jit(solution)/shard_map/all_gather | solution.py:22
  9.7 29.2 %copy-start.1 = (bf16[1,128,2048]{1,2,0:T(8,128)(2,1)}, bf16[1,128,2048]{1,2,0:T(8,128)(2,1)S(1)}, u32[]{:S(2)}) copy-start(bf16[1,128,2048]{1,2,0:T(8,128)(2,1)S(1)} %copy.44) | copy-start | bytes 1572868
  9.7 1.9 copy-start.4
  9.8 2.0 copy-start.3
  11.5 171.9 %reduce-scatter.2.cloned.1.call-start = ((), (), s32[]{:S(2)}) async-start(), calls=%async_computation.1 | async-start | bytes 1572864 | tf_op jit(solution)/shard_map/reduce_scatter | solution.py:127
  140.8 135.6 %all-reduce.2.cloned.1.call-start = ((), (), s32[]{:S(2)}) async-start(), calls=%async_computation.2 | async-start | bytes 1048576 | tf_op jit(solution)/shard_map/psum | solution.py:128
  183.4 220.8 %all-gather.8.cloned.1.call-start = ((), (), s32[]{:S(2)}) async-start(), calls=%async_computation.4 | async-start | bytes 17825792 | tf_op jit(solution)/shard_map/all_gather | solution.py:22
  426.8 1.0 copy-start.2
Sparse Core Ops, SparseCore 0:
  11.6 124.9 all-gather.5
  140.9 42.3 reduce-scatter.1
  186.8 89.6 all-reduce.1
  278.4 125.7 all-gather.7
where the time goes:
time: 437 us; the launch traced here: 436 us
  waiting for transfers between devices  354 us (81%)
  other arithmetic  26.4 us (6%)
  blocking collectives  26.2 us (6%)
  between operations  14 us (3%)
  matrix products  10.4 us (2%)
    all_gather x2, waiting for transfers between devices, entering(): gathered = jax.tree.map(lambda a: lax.all_gather(a, axis), part)  221 us
    psum x1, waiting for transfers between devices, on_device(): grad_rows = lax.psum(owner_grad, 'seq')  90.6 us
    reduce_scatter x1, waiting for transfers between devices, on_device(): lax.psum_scatter(partial_grad, 'dp', scatter_dimension=0, tiled=True)  42.5 us
    add x15, other arithmetic, pair_combine(): later_pair[0][:, None, None] * earlier_pair[1] + later_pair[1]  21.7 us
    all_gather x1, blocking collectives, entering(): gathered = jax.tree.map(lambda a: lax.all_gather(a, axis), part)  18.4 us
  transfers between devices with their start and end apart: 4, of which 4 were waited for; matrix products, arithmetic and copies ran while one was open for 2% of the time, Pallas kernels for 0%

commit v1 on v0

--- a/solution.py
+++ b/solution.py
@@ -125,7 +125,13 @@
     grad_half = write_grad.astype(jnp.bfloat16)
     partial_grad = jnp.dot(input_rows.T, grad_half, preferred_element_type=jnp.float32)
     owner_grad = lax.psum_scatter(partial_grad, "dp", scatter_dimension=0, tiled=True)
-    grad_rows = lax.psum(owner_grad, "seq")
+    count_2 = lax.axis_size("seq")
+    grad_rows, far = (owner_grad, 1)
+    while far < count_2:
+        grad_rows = grad_rows + lax.ppermute(
+            grad_rows, "seq", [(i, i ^ far) for i in range(count_2)]
+        )
+        far = 2 * far
     new_weight, new_first, new_second = adam_update(
         grad_rows, write_weight, first_moment, second_moment
     )

time: 437 us -> 370 us (0.85)
  waiting for transfers between devices: 354 us -> 284 us
    ppermute x0 -> x4, waiting for transfers between devices: none -> 113 us  [on_device(): lax.ppermute(grad_rows, 'seq', [(i, i ^ far) for i in range(count_2)])]
    all_gather x2, waiting for transfers between devices: 221 us -> 130 us  [entering(): gathered = jax.tree.map(lambda a: lax.all_gather(a, axis), part)]
    psum x1 -> x0, waiting for transfers between devices: 90.6 us -> none  [on_device(): grad_rows = lax.psum(owner_grad, 'seq')]
  transfers between devices with their start and end apart: 4 -> 7, of which waited for: 4 -> 7; matrix products, arithmetic and copies ran while one was open for 2% -> 3% of each run, Pallas kernels for 0% -> 0%
where the time goes in v1:
time: 370 us; the launch traced here: 369 us
  waiting for transfers between devices  284 us (77%)
  other arithmetic  27.7 us (7%)
  blocking collectives  26.2 us (7%)
  between operations  14 us (4%)
  matrix products  11.5 us (3%)
    all_gather x2, waiting for transfers between devices, entering(): gathered = jax.tree.map(lambda a: lax.all_gather(a, axis), part)  130 us
    ppermute x4, waiting for transfers between devices, on_device(): lax.ppermute(grad_rows, 'seq', [(i, i ^ far) for i in range(count_2)])  113 us
    reduce_scatter x1, waiting for transfers between devices, on_device(): lax.psum_scatter(partial_grad, 'dp', scatter_dimension=0, tiled=True)  40.7 us
    add x15, other arithmetic, pair_combine(): later_pair[0][:, None, None] * earlier_pair[1] + later_pair[1]  21.7 us
    all_gather x1, blocking collectives, entering(): gathered = jax.tree.map(lambda a: lax.all_gather(a, axis), part)  18.4 us
    all_gather x1, blocking collectives, on_device(): lax.all_gather(weight_half, 'dp', axis=0, tiled=True)  7.86 us
  transfers between devices with their start and end apart: 7, of which 7 were waited for; matrix products, arithmetic and copies ran while one was open for 3% of the time, Pallas kernels for 0%

profile of v1, /device:TPU:29, one launch (start us, length us, event | category | flops | bytes accessed | tf_op | source)
XLA Modules:
  0.0 368.8 jit_solution(12057582669305195632)
XLA Ops:
  7.2 1.4 copy.44
  9.8 1.6 fusion.17
  12.0 7.9 %all_gather.24 = bf16[4096,64]{0,1:T(8,128)(2,1)S(1)} all-gather(bf16[2048,64]{0,1:T(8,128)(2,1)S(1)} %convert_element_type.22), channel_id=1, replica_groups=mesh['seq'=16,'dp'=2] {'dp'}, dimensions={0}, use_global_device_ids=true | all-gather | bytes 786432 | tf_op jit(solution)/shard_map/all_gather | solution.py:71
  20.3 18.4 %all-gather.2 = f32[16,1,32]{2,1,0:T(1,128)S(1)} all-gather(f32[1,1,32]{2,1,0:T(1,128)S(1)} %get-tuple-element.175), channel_id=1, replica_groups=mesh['seq'=16,'dp'=2] {'seq'}, dimensions={0}, use_global_device_ids=true | all-gather | bytes 2176 | tf_op jit(solution)/shard_map/all_gather | solution.py:22
  38.9 1.8 fusion
  40.8 95.8 %all-gather.6.cloned.1.call-done = f32[512,64,64]{2,1,0:T(8,128)} async-done(((f32[32,64,64]{2,1,0:T(8,128)}), f32[512,64,64]{2,1,0:T(8,128)}) %all-gather.6.cloned.1.call-update) | async-done | bytes 8388624 | tf_op jit(solution)/shard_map/all_gather | solution.py:22
  137.4 1.9 fusion.7
  140.9 1.6 fusion.4
  142.6 40.7 %reduce-scatter.2.cloned.1.call-done = f32[2048,64]{0,1:T(8,128)} async-done(((f32[4096,64]{0,1:T(8,128)}), f32[2048,64]{0,1:T(8,128)}) %reduce-scatter.2.cloned.1.call-update) | async-done | bytes 524304 | tf_op jit(solution)/shard_map/reduce_scatter | solution.py:127
  184.2 1.7 collective-permute-done
  187.4 17.0 %collective-permute-done.1 = f32[2048,64]{0,1:T(8,128)S(1)} collective-permute-done((f32[2048,64]{0,1:T(8,128)S(1)}, f32[2048,64]{0,1:T(8,128)S(1)}, u32[]{:S(2)}, u32[]{:S(2)}) %collective-permute-start.1) | collective-permute-done | bytes 524320 | tf_op jit(solution)/shard_map/ppermute | solution.py:131
  204.8 36.5 %collective-permute-done.2 = f32[2048,64]{0,1:T(8,128)S(1)} collective-permute-done((f32[2048,64]{0,1:T(8,128)S(1)}, f32[2048,64]{0,1:T(8,128)S(1)}, u32[]{:S(2)}, u32[]{:S(2)}) %collective-permute-start.2) | collective-permute-done | bytes 524320 | tf_op jit(solution)/shard_map/ppermute | solution.py:131
  242.1 58.0 %collective-permute-done.3 = f32[2048,64]{0,1:T(8,128)} collective-permute-done((f32[2048,64]{0,1:T(8,128)S(1)}, f32[2048,64]{0,1:T(8,128)}, u32[]{:S(2)}, u32[]{:S(2)}) %collective-permute-start.3) | collective-permute-done | bytes 524320 | tf_op jit(solution)/shard_map/ppermute | solution.py:131
  300.0 2.8 multiply_subtract_fusion
  302.8 33.8 %all-gather.8.cloned.1.call-done = f32[512,64,64]{2,1,0:T(8,128)} async-done(((f32[32,64,64]{2,1,0:T(8,128)}), f32[512,64,64]{2,1,0:T(8,128)}) %all-gather.8.cloned.1.call-update) | async-done | bytes 8388624 | tf_op jit(solution)/shard_map/all_gather | solution.py:22
  336.7 22.4 %while.27 = (s32[]{:T(128)}, f32[32,64,64]{2,1,0:T(8,128)S(1)}, s32[]{:T(128)}, f32[16,32]{1,0:T(8,128)S(1)}, f32[16,32,64,64]{3,2,1,0:T(8,128)}, /*index=5*/s32[]{:T(128)}, s32[]{:T(128)}, s32[]{:T(128)}) while((s32[]{:T(128)}, f32[32,64,64]{2,1,0:T(8,128)S(1)}, s32[]{:T(128)}, f32[16,32]{1,0:T(8,128)S(1)}, f32[16,32,64,64]{3,2,1,0:T(8,128)}, ...), condition=%wide.region_4.5_spmd, body=%wide.region_3.4_spmd.sunk | while | flops 262149 | bytes 1573383 | solution.py:31
  336.8 1.4 bitcast_add_fusion.5
  338.3 1.4 bitcast_add_fusion.5
  339.7 1.4 bitcast_add_fusion.5
  341.2 1.4 bitcast_add_fusion.5
  342.7 1.4 bitcast_add_fusion.5
  344.2 1.4 bitcast_add_fusion.5
  345.7 1.4 bitcast_add_fusion.5
  347.2 1.4 bitcast_add_fusion.5
  348.7 1.4 bitcast_add_fusion.5
  350.2 1.4 bitcast_add_fusion.5
  351.7 1.4 bitcast_add_fusion.5
  353.2 1.4 bitcast_add_fusion.5
  354.7 1.4 bitcast_add_fusion.5
  356.2 1.4 bitcast_add_fusion.5
  357.6 1.4 bitcast_add_fusion.5
  359.1 1.7 fusion.6
  (74 shorter events, 10.1 us)
Async XLA Ops:
  7.2 12.7 %copy-start = (bf16[1,128,4096]{2,1,0:T(8,128)(2,1)S(1)}, bf16[1,128,4096]{2,1,0:T(8,128)(2,1)}, u32[]{:S(2)}) copy-start(bf16[1,128,4096]{2,1,0:T(8,128)(2,1)} %param.12) | copy-start | bytes 3145732
  7.2 2.7 copy-start.4
  7.2 129.4 %all-gather.6.cloned.1.call-start = ((), (), s32[]{:S(2)}) async-start(), calls=%async_computation.2 | async-start | bytes 17825792 | tf_op jit(solution)/shard_map/all_gather | solution.py:22
  8.6 30.3 %copy-start.1 = (bf16[1,128,2048]{1,2,0:T(8,128)(2,1)}, bf16[1,128,2048]{1,2,0:T(8,128)(2,1)S(1)}, u32[]{:S(2)}) copy-start(bf16[1,128,2048]{1,2,0:T(8,128)(2,1)S(1)} %copy.44) | copy-start | bytes 1572868
  9.7 1.9 copy-start.2
  9.8 1.8 copy-start.3
  11.5 171.9 %reduce-scatter.2.cloned.1.call-start = ((), (), s32[]{:S(2)}) async-start(), calls=%async_computation.1 | async-start | bytes 1572864 | tf_op jit(solution)/shard_map/reduce_scatter | solution.py:127
  140.9 195.7 %all-gather.8.cloned.1.call-start = ((), (), s32[]{:S(2)}) async-start(), calls=%async_computation.3 | async-start | bytes 17825792 | tf_op jit(solution)/shard_map/all_gather | solution.py:22
  183.3 2.6 collective-permute-start
  187.0 17.3 %collective-permute-start.1 = (f32[2048,64]{0,1:T(8,128)S(1)}, f32[2048,64]{0,1:T(8,128)S(1)}, u32[]{:S(2)}, u32[]{:S(2)}) collective-permute-start(f32[2048,64]{0,1:T(8,128)S(1)} %add.93), channel_id=1, source_target_pairs={{0,4},{2,6},{4,0},{6,2},{8,12},{10,14},{12,8},{14,10},{16,20},{18,... | collective-permute-start | bytes 1572872 | tf_op jit(solution)/shard_map/ppermute | solution.py:131
  204.4 36.8 %collective-permute-start.2 = (f32[2048,64]{0,1:T(8,128)S(1)}, f32[2048,64]{0,1:T(8,128)S(1)}, u32[]{:S(2)}, u32[]{:S(2)}) collective-permute-start(f32[2048,64]{0,1:T(8,128)S(1)} %add.94), channel_id=1, source_target_pairs={{0,8},{2,10},{4,12},{6,14},{8,0},{10,2},{12,4},{14,6},{16,24},{18,... | collective-permute-start | bytes 1572872 | tf_op jit(solution)/shard_map/ppermute | solution.py:131
  241.3 58.8 %collective-permute-start.3 = (f32[2048,64]{0,1:T(8,128)S(1)}, f32[2048,64]{0,1:T(8,128)}, u32[]{:S(2)}, u32[]{:S(2)}) collective-permute-start(f32[2048,64]{0,1:T(8,128)S(1)} %add.95), channel_id=1, source_target_pairs={{0,16},{2,18},{4,20},{6,22},{8,24},{10,26},{12,28},{14,30},{16,0},... | collective-permute-start | bytes 1572872 | tf_op jit(solution)/shard_map/ppermute | solution.py:131
Sparse Core Ops, SparseCore 0:
  11.6 124.9 all-gather.5
  141.0 42.2 reduce-scatter.1
  185.5 151.0 all-gather.7
